TPU v7x, 32 devices: a whole 2x2x4 slice. The times are simulated.
32 devices in a mesh: rep: 16 (over z, x, core), grp: 2 (over y).
Axes of the slice: x: 2, y: 2, z: 4, core: 2. Of those that a mesh axis runs over, the one named last changes fastest.
Arguments:
- stream_in: float32 [16, 256, 1024], P('rep', 'grp'), may hold values from -6 to 6
- first_norm_gain: bfloat16 [1024], P('grp'), may hold values from 0.099609375 to 1.8984375
- first_norm_bias: bfloat16 [1024], P('grp'), may hold values from -3 to 3
- w_qkv: bfloat16 [1024, 3072], P('grp'), may hold values from -6 to 6, as said below
- bias_q: bfloat16 [1024], P('grp'), may hold values from -3 to 3
- bias_v: bfloat16 [1024], P('grp'), may hold values from -3 to 3
- w_out: bfloat16 [1024, 1024], P('grp'), may hold values from -0.75 to 0.75
- bias_out: bfloat16 [1024], P('grp'), may hold values from -3 to 3
- second_norm_gain: bfloat16 [1024], P('grp'), may hold values from 0.099609375 to 1.8984375
- second_norm_bias: bfloat16 [1024], P('grp'), may hold values from -3 to 3
- w_up: bfloat16 [1024, 4096], P('grp'), may hold values from -0.1875 to 0.1875
- bias_up: bfloat16 [4096], P('grp'), may hold values from -3 to 3
- w_down: bfloat16 [4096, 1024], P('grp'), may hold values from -0.09375 to 0.09375
- bias_down: bfloat16 [1024], P('grp'), may hold values from -3 to 3
- cotangent: float32 [16, 256, 1024], P('rep', 'grp'), may hold values from -6 to 6
Outputs:
- stream_out: float32 [16, 256, 1024], P('rep', 'grp')
- stream_grad: float32 [16, 256, 1024], P('rep', 'grp')
- ln1_gain_grad: float32 [1024], P('grp')
- ln1_bias_grad: float32 [1024], P('grp')
- w_qkv_grad: float32 [1024, 3072], P('grp')
- bias_q_grad: float32 [1024], P('grp')
- bias_v_grad: float32 [1024], P('grp')
- w_out_grad: float32 [1024, 1024], P('grp')
- bias_out_grad: float32 [1024], P('grp')
- ln2_gain_grad: float32 [1024], P('grp')
- ln2_bias_grad: float32 [1024], P('grp')
- w_up_grad: float32 [1024, 4096], P('grp')
- bias_up_grad: float32 [4096], P('grp')
- w_down_grad: float32 [4096, 1024], P('grp')
- bias_down_grad: float32 [1024], P('grp')
Inputs may be any that keep to these rules, and one draw needn't show every extreme that they name: `w_qkv`: the columns hold the query, key and value projections in that order.
All inputs are finite; a program needn't handle non-finite values.
Results may differ from a plain program's by a relative error of at most 0.018.
Values may be sent and summed in bfloat16 or wider, within the bound.
A program may use at most 192 MiB of HBM per device.

v0:
```python
import math

import jax
import jax.numpy as jnp
from jax import lax
from jax.sharding import PartitionSpec as P

HEADS = 16
HEAD_DIM = 64


NORM_EPS = 1e-05
GELU_COEF = math.sqrt(2.0 / math.pi)


def layer_norm_forward(residual_state, norm_gain, norm_shift):
    center = residual_state - jnp.mean(residual_state, axis=-1, keepdims=True)
    inv_std = lax.rsqrt(jnp.mean(center * center, axis=-1, keepdims=True) + NORM_EPS)
    normed = center * inv_std
    return (
        normed * norm_gain.astype(jnp.float32) + norm_shift.astype(jnp.float32),
        normed,
        inv_std,
    )


def layer_norm_backward(grad_norm, normed, inv_std, norm_gain):
    scaled = grad_norm * norm_gain.astype(jnp.float32)
    return inv_std * (
        scaled
        - jnp.mean(scaled, axis=-1, keepdims=True)
        - normed * jnp.mean(scaled * normed, axis=-1, keepdims=True)
    )


def gelu_parts(pre_act):
    inner_arg = GELU_COEF * (pre_act + 0.044715 * pre_act * pre_act * pre_act)
    tangent = jnp.tanh(inner_arg)
    gelu_value = 0.5 * pre_act * (1.0 + tangent)
    gelu_slope = 0.5 * (1.0 + tangent) + 0.5 * pre_act * (1.0 - tangent * tangent) * GELU_COEF * (
        1.0 + 3.0 * 0.044715 * pre_act * pre_act
    )
    return (gelu_value, gelu_slope)


def split_heads(matrix):
    return matrix.reshape(matrix.shape[0], HEADS, HEAD_DIM)


def masked_scores(queries, keys_all, first_row):
    raw_scores = jnp.einsum(
        "qhd,khd->hqk",
        split_heads(queries),
        split_heads(keys_all),
        preferred_element_type=jnp.float32,
    ) * HEAD_DIM ** (-0.5)
    query_pos = first_row + jnp.arange(queries.shape[0], dtype=jnp.int32)
    key_pos = jnp.arange(keys_all.shape[0], dtype=jnp.int32)
    allowed = key_pos[None, :] <= query_pos[:, None]
    return jnp.where(allowed[None], raw_scores, jnp.float32(-1e30))


def attend_forward(queries, keys_all, values_all, first_row):
    scores = masked_scores(queries, keys_all, first_row)
    row_max = jnp.max(scores, axis=-1, keepdims=True)
    log_total = row_max + jnp.log(jnp.sum(jnp.exp(scores - row_max), axis=-1, keepdims=True))
    prob_b = jnp.exp(scores - log_total).astype(jnp.bfloat16)
    context = jnp.einsum(
        "hqk,khd->qhd", prob_b, split_heads(values_all), preferred_element_type=jnp.float32
    )
    return (context.reshape(queries.shape[0], -1).astype(jnp.bfloat16), log_total)


def attend_backward(queries, keys_all, values_all, grad_context, log_total, first_row):
    scores = masked_scores(queries, keys_all, first_row)
    attn_prob = jnp.exp(scores - log_total)
    prob_b = attn_prob.astype(jnp.bfloat16)
    grad_prob = jnp.einsum(
        "qhd,khd->hqk",
        split_heads(grad_context),
        split_heads(values_all),
        preferred_element_type=jnp.float32,
    )
    grad_score = (
        attn_prob
        * (grad_prob - jnp.sum(attn_prob * grad_prob, axis=-1, keepdims=True))
        * HEAD_DIM ** (-0.5)
    ).astype(jnp.bfloat16)
    grad_queries = jnp.einsum(
        "hqk,khd->qhd", grad_score, split_heads(keys_all), preferred_element_type=jnp.float32
    )
    grad_keys = jnp.einsum(
        "hqk,qhd->khd", grad_score, split_heads(queries), preferred_element_type=jnp.float32
    )
    grad_values = jnp.einsum(
        "hqk,qhd->khd", prob_b, split_heads(grad_context), preferred_element_type=jnp.float32
    )
    local_rows = queries.shape[0]
    all_rows = keys_all.shape[0]
    return (
        grad_queries.reshape(local_rows, -1),
        grad_keys.reshape(all_rows, -1),
        grad_values.reshape(all_rows, -1),
    )


def owned_product(columns, full_rows):
    return jnp.dot(columns.T, full_rows, preferred_element_type=jnp.float32)


def per_device(
    stream_in,
    first_norm_gain,
    first_norm_bias,
    w_qkv,
    bias_q,
    bias_v,
    w_out,
    bias_out,
    second_norm_gain,
    second_norm_bias,
    w_up,
    bias_up,
    w_down,
    bias_down,
    cotangent,
):
    gathered = (
        lax.all_gather(first_norm_gain, "grp", axis=0, tiled=True),
        lax.all_gather(first_norm_bias, "grp", axis=0, tiled=True),
        lax.all_gather(w_qkv, "grp", axis=0, tiled=True),
        lax.all_gather(bias_q, "grp", axis=0, tiled=True),
        lax.all_gather(bias_v, "grp", axis=0, tiled=True),
        lax.all_gather(w_out, "grp", axis=0, tiled=True),
        lax.all_gather(bias_out, "grp", axis=0, tiled=True),
        lax.all_gather(second_norm_gain, "grp", axis=0, tiled=True),
        lax.all_gather(second_norm_bias, "grp", axis=0, tiled=True),
        lax.all_gather(w_up, "grp", axis=0, tiled=True),
        lax.all_gather(bias_up, "grp", axis=0, tiled=True),
        lax.all_gather(w_down, "grp", axis=0, tiled=True),
        lax.all_gather(bias_down, "grp", axis=0, tiled=True),
    )
    (
        gathered_first_gain,
        gathered_first_bias,
        full_wqkv,
        full_bq,
        full_bv,
        full_wo,
        full_bo,
        gathered_second_gain,
        gathered_second_bias,
        full_wu,
        full_bu,
        full_wd,
        full_bd,
    ) = gathered
    residual_state = stream_in[0]
    output_gradient = cotangent[0]
    rows = residual_state.shape[0]
    width = residual_state.shape[1]
    first_row = lax.axis_index("grp") * rows
    first_normalized, first_standardized, first_inverse_deviation = layer_norm_forward(
        residual_state, gathered_first_gain, gathered_first_bias
    )
    act_one = first_normalized.astype(jnp.bfloat16)
    projected = jnp.dot(act_one, full_wqkv, preferred_element_type=jnp.float32)
    queries = (projected[:, :width] + full_bq.astype(jnp.float32)).astype(jnp.bfloat16)
    keys_local = projected[:, width : 2 * width].astype(jnp.bfloat16)
    values_local = (projected[:, 2 * width :] + full_bv.astype(jnp.float32)).astype(jnp.bfloat16)
    keys_all, values_all = (
        lax.all_gather(keys_local, "grp", axis=0, tiled=True),
        lax.all_gather(values_local, "grp", axis=0, tiled=True),
    )
    context, log_total = attend_forward(queries, keys_all, values_all, first_row)
    midpoint_state = (
        residual_state
        + jnp.dot(context, full_wo, preferred_element_type=jnp.float32)
        + full_bo.astype(jnp.float32)
    )
    second_normalized, second_standardized, second_inverse_deviation = layer_norm_forward(
        midpoint_state, gathered_second_gain, gathered_second_bias
    )
    act_two = second_normalized.astype(jnp.bfloat16)
    pre_act = jnp.dot(act_two, full_wu, preferred_element_type=jnp.float32) + full_bu.astype(
        jnp.float32
    )
    gelu_value, gelu_slope = gelu_parts(pre_act)
    hidden = gelu_value.astype(jnp.bfloat16)
    result = (
        midpoint_state
        + jnp.dot(hidden, full_wd, preferred_element_type=jnp.float32)
        + full_bd.astype(jnp.float32)
    )
    back_keys, back_values = (keys_all, values_all)
    (
        backward_first_gain,
        back_b1,
        back_wqkv,
        back_bq,
        back_bv,
        back_wo,
        back_bo,
        backward_second_gain,
        back_b2,
        back_wu,
        back_bu,
        back_wd,
        back_bd,
    ) = gathered
    cot_b = output_gradient.astype(jnp.bfloat16)
    d_bias_down = jnp.sum(output_gradient, axis=0)
    grad_pre = jnp.dot(cot_b, back_wd.T, preferred_element_type=jnp.float32) * gelu_slope
    grad_pre_b = grad_pre.astype(jnp.bfloat16)
    d_bias_up = jnp.sum(grad_pre, axis=0)
    second_activation_gradient = jnp.dot(grad_pre_b, back_wu.T, preferred_element_type=jnp.float32)
    second_norm_gain_gradient = jnp.sum(second_activation_gradient * second_standardized, axis=0)
    d_ln2_bias = jnp.sum(second_activation_gradient, axis=0)
    act_two_cols, hidden_cols = (
        lax.all_to_all(act_two, "grp", split_axis=1, concat_axis=0, tiled=True),
        lax.all_to_all(hidden, "grp", split_axis=1, concat_axis=0, tiled=True),
    )
    cot_full, grad_pre_full = (
        lax.all_gather(cot_b, "grp", axis=0, tiled=True),
        lax.all_gather(grad_pre_b, "grp", axis=0, tiled=True),
    )
    small_two = (
        lax.psum_scatter(second_norm_gain_gradient, "grp", scatter_dimension=0, tiled=True),
        lax.psum_scatter(d_ln2_bias, "grp", scatter_dimension=0, tiled=True),
        lax.psum_scatter(d_bias_up, "grp", scatter_dimension=0, tiled=True),
        lax.psum_scatter(d_bias_down, "grp", scatter_dimension=0, tiled=True),
    )
    mlp_shares = (
        small_two[0],
        small_two[1],
        owned_product(act_two_cols, grad_pre_full),
        small_two[2],
        owned_product(hidden_cols, cot_full),
        small_two[3],
    )
    midpoint_gradient = output_gradient + layer_norm_backward(
        second_activation_gradient,
        second_standardized,
        second_inverse_deviation,
        backward_second_gain,
    )
    grad_mid_b = midpoint_gradient.astype(jnp.bfloat16)
    d_bias_out = jnp.sum(midpoint_gradient, axis=0)
    grad_context = jnp.dot(grad_mid_b, back_wo.T, preferred_element_type=jnp.float32).astype(
        jnp.bfloat16
    )
    grad_queries, grad_keys_all, grad_values_all = attend_backward(
        queries, back_keys, back_values, grad_context, log_total, first_row
    )
    grad_keys, grad_values = (
        lax.psum_scatter(
            grad_keys_all.astype(jnp.bfloat16), "grp", scatter_dimension=0, tiled=True
        ).astype(jnp.float32),
        lax.psum_scatter(
            grad_values_all.astype(jnp.bfloat16), "grp", scatter_dimension=0, tiled=True
        ).astype(jnp.float32),
    )
    d_bias_q = jnp.sum(grad_queries, axis=0)
    d_bias_v = jnp.sum(grad_values, axis=0)
    grad_proj = jnp.concatenate([grad_queries, grad_keys, grad_values], axis=1).astype(jnp.bfloat16)
    first_activation_gradient = jnp.dot(grad_proj, back_wqkv.T, preferred_element_type=jnp.float32)
    first_norm_gain_gradient = jnp.sum(first_activation_gradient * first_standardized, axis=0)
    d_ln1_bias = jnp.sum(first_activation_gradient, axis=0)
    input_gradient = midpoint_gradient + layer_norm_backward(
        first_activation_gradient, first_standardized, first_inverse_deviation, backward_first_gain
    )
    act_one_cols, context_cols = (
        lax.all_to_all(act_one, "grp", split_axis=1, concat_axis=0, tiled=True),
        lax.all_to_all(context, "grp", split_axis=1, concat_axis=0, tiled=True),
    )
    mid_full, proj_full = (
        lax.all_gather(grad_mid_b, "grp", axis=0, tiled=True),
        lax.all_gather(grad_proj, "grp", axis=0, tiled=True),
    )
    small_one = (
        lax.psum_scatter(first_norm_gain_gradient, "grp", scatter_dimension=0, tiled=True),
        lax.psum_scatter(d_ln1_bias, "grp", scatter_dimension=0, tiled=True),
        lax.psum_scatter(d_bias_q, "grp", scatter_dimension=0, tiled=True),
        lax.psum_scatter(d_bias_v, "grp", scatter_dimension=0, tiled=True),
        lax.psum_scatter(d_bias_out, "grp", scatter_dimension=0, tiled=True),
    )
    attn_shares = (
        small_one[0],
        small_one[1],
        owned_product(act_one_cols, proj_full),
        small_one[2],
        small_one[3],
        owned_product(context_cols, mid_full),
        small_one[4],
    )
    totals = (
        lax.psum(attn_shares[0].astype(jnp.bfloat16), "rep").astype(jnp.float32),
        lax.psum(attn_shares[1].astype(jnp.bfloat16), "rep").astype(jnp.float32),
        lax.psum(attn_shares[2].astype(jnp.bfloat16), "rep").astype(jnp.float32),
        lax.psum(attn_shares[3].astype(jnp.bfloat16), "rep").astype(jnp.float32),
        lax.psum(attn_shares[4].astype(jnp.bfloat16), "rep").astype(jnp.float32),
        lax.psum(attn_shares[5].astype(jnp.bfloat16), "rep").astype(jnp.float32),
        lax.psum(attn_shares[6].astype(jnp.bfloat16), "rep").astype(jnp.float32),
        lax.psum(mlp_shares[0].astype(jnp.bfloat16), "rep").astype(jnp.float32),
        lax.psum(mlp_shares[1].astype(jnp.bfloat16), "rep").astype(jnp.float32),
        lax.psum(mlp_shares[2].astype(jnp.bfloat16), "rep").astype(jnp.float32),
        lax.psum(mlp_shares[3].astype(jnp.bfloat16), "rep").astype(jnp.float32),
        lax.psum(mlp_shares[4].astype(jnp.bfloat16), "rep").astype(jnp.float32),
        lax.psum(mlp_shares[5].astype(jnp.bfloat16), "rep").astype(jnp.float32),
    )
    return (
        result[None],
        input_gradient[None],
        totals[0],
        totals[1],
        totals[2],
        totals[3],
        totals[4],
        totals[5],
        totals[6],
        totals[7],
        totals[8],
        totals[9],
        totals[10],
        totals[11],
        totals[12],
    )


def solution(mesh):
    return jax.shard_map(
        per_device,
        mesh=mesh,
        in_specs=(
            P("rep", "grp", None),
            P("grp"),
            P("grp"),
            P("grp", None),
            P("grp"),
            P("grp"),
            P("grp", None),
            P("grp"),
            P("grp"),
            P("grp"),
            P("grp", None),
            P("grp"),
            P("grp", None),
            P("grp"),
            P("rep", "grp", None),
        ),
        out_specs=(
            P("rep", "grp", None),
            P("rep", "grp", None),
            P("grp"),
            P("grp"),
            P("grp", None),
            P("grp"),
            P("grp"),
            P("grp", None),
            P("grp"),
            P("grp"),
            P("grp"),
            P("grp", None),
            P("grp"),
            P("grp", None),
            P("grp"),
        ),
        check_vma=False,
    )
```

profile of v0, /device:TPU:0, one launch (start us, length us, event | category | flops | bytes accessed | tf_op | source)
XLA Modules:
  0.0 757.3 jit_solution(12916975851959377282)
XLA Ops:
  10.2 5.3 all-gather.4
  15.5 4.4 all-gather.1
  19.9 4.4 all-gather
  24.3 4.6 all-gather.3
  28.9 4.5 all-gather.2
  33.4 4.6 all_gather.69
  38.0 4.5 all-gather.6
  42.6 4.5 all-gather.5
  48.4 44.5 %all-gather.15.cloned.1.call-done = bf16[1024,3072]{1,0:T(8,128)(2,1)} async-done(((bf16[512,3072]{1,0:T(8,128)(2,1)}), bf16[1024,3072]{1,0:T(8,128)(2,1)}) %all-gather.15.cloned.1.call-update) | async-done | bytes 6291472 | tf_op jit(solution)/shard_map/all_gather | solution.py:131
  92.9 3.9 fusion.36
  96.9 9.6 %all_gather.61 = bf16[256,1024]{1,0:T(8,128)(2,1)S(1)} all-gather(bf16[128,1024]{1,0:T(8,128)(2,1)S(1)} %get-tuple-element.50), channel_id=1, replica_groups=mesh['rep'=16,'grp'=2] {'grp'}, dimensions={0}, use_global_device_ids=true | all-gather | bytes 786432 | tf_op jit(solution)/shard_map/all_gather | solution.py:173
  106.9 14.6 %all_gather.63 = bf16[256,1024]{1,0:T(8,128)(2,1)S(1)} all-gather(bf16[128,1024]{1,0:T(8,128)(2,1)S(1)} %slice.23), channel_id=1, replica_groups=mesh['rep'=16,'grp'=2] {'grp'}, dimensions={0}, use_global_device_ids=true | all-gather | bytes 786432 | tf_op jit(solution)/shard_map/all_gather | solution.py:172
  121.5 1.0 copy.56
  122.5 1.6 fusion.50
  125.4 8.4 %all-gather.17.cloned.1.call-done = bf16[1024,1024]{1,0:T(8,128)(2,1)} async-done(((bf16[512,1024]{1,0:T(8,128)(2,1)}), bf16[1024,1024]{1,0:T(8,128)(2,1)}) %all-gather.17.cloned.1.call-update) | async-done | bytes 2097168 | tf_op jit(solution)/shard_map/all_gather | solution.py:134
  133.8 2.1 fusion.51
  136.1 0.9 add_convert_fusion.1
  137.0 102.3 %all-gather.19.cloned.1.call-done = bf16[1024,4096]{1,0:T(8,128)(2,1)} async-done(((bf16[512,4096]{1,0:T(8,128)(2,1)}), bf16[1024,4096]{1,0:T(8,128)(2,1)}) %all-gather.19.cloned.1.call-update) | async-done | bytes 8388624 | tf_op jit(solution)/shard_map/all_gather | solution.py:138
  239.4 7.1 multiply_convert_fusion.1
  246.4 98.4 %all-gather.21.cloned.1.call-done = bf16[4096,1024]{1,0:T(8,128)(2,1)} async-done(((bf16[2048,1024]{1,0:T(8,128)(2,1)}), bf16[4096,1024]{1,0:T(8,128)(2,1)}) %all-gather.21.cloned.1.call-update) | async-done | bytes 8388624 | tf_op jit(solution)/shard_map/all_gather | solution.py:140
  344.8 8.5 %fusion.47 = (f32[4096]{0:T(1024)S(1)}, bf16[128,4096]{1,0:T(8,128)(2,1)}) fusion(f32[128,4096]{1,0:T(8,128)} %get-tuple-element.60, bf16[128,1024]{1,0:T(8,128)(2,1)S(1)} %copy-done.17, bf16[4096,1024]{1,0:T(8,128)(2,1)} %all-gather.21.cloned.1.call-done), kind=kOutput, calls=%fused_computation.97 | convolution fusion | flops 1084223488 | bytes 11812864 | tf_op jit(solution)/shard_map/dot_general | solution.py:213
  353.2 6.8 multiply_reduce_fusion.1
  360.3 0.8 copy-done.3
  361.8 1.6 convolution_convert_fusion.5
  363.4 1.8 copy.57
  365.2 2.3 convolution_convert_fusion.4
  367.5 2.0 copy.65
  369.8 2.9 fusion.54
  372.8 14.4 %fusion.16 = bf16[16,64,256]{2,1,0:T(8,128)(2,1)} fusion(bf16[128,16,64]{0,2,1:T(8,128)(2,1)} %bitcast.125, f32[16,128,256]{2,1,0:T(8,128)} %fusion.54, f32[16,128,256]{2,1,0:T(8,128)S(1)} %get-tuple-element.56, f32[16,128]{1,0:T(8,128)S(1)} %log_add_fusion), kind=kOutput, calls=%fused_computation.24 | convolution fusion | flops 71043328 | bytes 4988928 | tf_op jit(solution)/shard_map/hqk,qhd->khd/dot_general | solution.py:92
  387.2 2.0 copy.63
  390.1 1.0 copy.58
  391.1 14.7 %fusion.49 = (f32[16,64]{1,0:T(8,128)S(1)}, bf16[128,16,64]{0,2,1:T(8,128)(2,1)}) fusion(bf16[256,16,64]{0,2,1:T(8,128)(2,1)} %bitcast.121, f32[16,128,256]{2,1,0:T(8,128)} %fusion.54, f32[16,128,256]{2,1,0:T(8,128)S(1)} %get-tuple-element.56, f32[16,128]{1,0:T(8,128)S(1)} %log_add_fusion), kind=kOutput, calls=%fused_computation.99 | convolution fusion | flops 71042304 | bytes 4993024 | tf_op jit(solution)/shard_map/hqk,khd->qhd/dot_general | solution.py:89
  405.8 1.2 copy.66
  407.0 1.9 copy.64
  408.9 2.0 pad_maximum_fusion
  411.0 1.0 add_convert_fusion
  412.1 3.5 all-to-all-start
  415.5 0.9 copy.60
  416.4 8.1 %all-to-all-done = bf16[128,2,512]{0,2,1:T(8,128)(2,1)S(1)} async-done(((bf16[128,2,512]{0,2,1:T(8,128)(2,1)}), bf16[128,2,512]{0,2,1:T(8,128)(2,1)S(1)}, u32[]{:S(2)}, u32[]{:S(2)}) %all-to-all-start) | async-done | bytes 262176 | tf_op jit(solution)/shard_map/all_to_all | solution.py:273
  424.5 3.4 all-to-all-start.1
  428.0 1.0 copy.75
  429.0 7.7 %all-to-all-done.1 = bf16[128,2,512]{2,0,1:T(8,128)(2,1)S(1)} async-done(((bf16[128,2,512]{2,0,1:T(8,128)(2,1)}), bf16[128,2,512]{2,0,1:T(8,128)(2,1)S(1)}, u32[]{:S(2)}, u32[]{:S(2)}) %all-to-all-start.1) | async-done | bytes 262176 | tf_op jit(solution)/shard_map/all_to_all | solution.py:274
  436.6 3.6 all-to-all-start.3
  440.2 23.4 %all_gather.75 = bf16[256,1024]{1,0:T(8,128)(2,1)S(1)} all-gather(bf16[128,1024]{1,0:T(8,128)(2,1)S(1)} %copy-done.18), channel_id=1, replica_groups=mesh['rep'=16,'grp'=2] {'grp'}, dimensions={0}, use_global_device_ids=true | all-gather | bytes 786432 | tf_op jit(solution)/shard_map/all_gather | solution.py:224
  463.6 1.8 copy.59
  465.5 1.7 copy.76
  467.1 14.4 %all_gather.73 = bf16[256,1024]{1,0:T(8,128)(2,1)S(1)} all-gather(bf16[128,1024]{1,0:T(8,128)(2,1)S(1)} %convert_element_type.202), channel_id=1, replica_groups=mesh['rep'=16,'grp'=2] {'grp'}, dimensions={0}, use_global_device_ids=true | all-gather | bytes 786432 | tf_op jit(solution)/shard_map/all_gather | solution.py:277
  481.5 2.4 convolution_convert_fusion.3
  483.9 3.4 all-to-all-start.2
  487.7 3.3 convolution_convert_fusion.2
  491.0 1.5 all-to-all-done.2
  492.5 4.9 convolution_convert_fusion
  497.5 4.1 convolution_convert_fusion.1
  502.2 4.4 all-gather.7
  508.6 5.9 fusion.24
  514.7 3.1 multiply_reduce_fusion.2
  517.8 7.5 all-reduce.9
  525.8 61.0 %all-reduce.10 = (bf16[512]{0:T(512)(128)(2,1)S(1)}, bf16[512]{0:T(512)(128)(2,1)S(1)}, bf16[512]{0:T(512)(128)(2,1)S(1)}, bf16[512]{0:T(512)(128)(2,1)S(1)}, bf...) all-reduce(bf16[512]{0:T(512)(128)(2,1)S(1)} %dynamic-slice.35, ...), channel_id=1, replica_groups=mesh['rep'=16,'grp'=2] {'rep'}, use_global_device_ids=true, to_apply=%region_15.16 | all-reduce | flops 6144 | bytes 24576 | tf_op jit(solution)/shard_map/psum | solution.py:297
  592.1 2.1 add_bitcast_fusion
  594.2 140.6 %all-reduce.14.cloned.1.call-done = (bf16[512,3072]{1,0:T(8,128)(2,1)}, bf16[512,1024]{1,0:T(8,128)(2,1)}, bf16[512,4096]{1,0:T(8,128)(2,1)}, bf16[2048,1024]{1,0:T(8,128)(2,1)}) async-done(((bf16[512,3072]{1,0:T(8,128)(2,1)}, bf16[512,1024]{1,0:T(8,128)(2,1)}, bf16[512,4096]{1,0:T(8,128)(2,1)}, bf16[2048,1024]{1,0:T(8,128)(2,1)}), (bf16[512,3072]{1,0:T(8,128)(2,1)}, bf16[512,1024]{1,0:T(8,128)(2,1)}, ...) | async-done | bytes 12582928 | tf_op jit(solution)/shard_map/psum | solution.py:299
  734.7 5.5 convert_element_type.217
  740.3 1.6 convert_element_type.225
  741.8 4.5 convert_element_type.233
  746.3 4.4 convert_element_type.237
  (157 shorter events, 15.8 us)
Async XLA Ops:
  7.2 85.7 %all-gather.15.cloned.1.call-start = ((), (), s32[]{:S(2)}) async-start(), calls=%async_computation.6 | async-start | bytes 9437184 | tf_op jit(solution)/shard_map/all_gather | solution.py:131
  7.9 125.9 %all-gather.17.cloned.1.call-start = ((), (), s32[]{:S(2)}) async-start(), calls=%async_computation.7 | async-start | bytes 3145728 | tf_op jit(solution)/shard_map/all_gather | solution.py:134
  8.7 230.7 %all-gather.19.cloned.1.call-start = ((), (), s32[]{:S(2)}) async-start(), calls=%async_computation.8 | async-start | bytes 12582912 | tf_op jit(solution)/shard_map/all_gather | solution.py:138
  9.4 0.7 copy-start.25
  9.4 6.1 copy-start.26
  9.4 10.4 %copy-start.27 = (bf16[512]{0:T(512)(128)(2,1)S(1)}, bf16[512]{0:T(512)(128)(2,1)}, u32[]{:S(2)}) copy-start(bf16[512]{0:T(512)(128)(2,1)} %param.16) | copy-start | bytes 3076
  9.4 14.8 %copy-start.28 = (bf16[512]{0:T(512)(128)(2,1)S(1)}, bf16[512]{0:T(512)(128)(2,1)}, u32[]{:S(2)}) copy-start(bf16[512]{0:T(512)(128)(2,1)} %param.19) | copy-start | bytes 3076
  9.4 19.4 %copy-start.29 = (bf16[512]{0:T(512)(128)(2,1)S(1)}, bf16[512]{0:T(512)(128)(2,1)}, u32[]{:S(2)}) copy-start(bf16[512]{0:T(512)(128)(2,1)} %param.20) | copy-start | bytes 3076
  9.5 24.0 %copy-start.24 = (bf16[2048]{0:T(1024)(128)(2,1)S(1)}, bf16[2048]{0:T(1024)(128)(2,1)}, u32[]{:S(2)}) copy-start(bf16[2048]{0:T(1024)(128)(2,1)} %param.26) | copy-start | bytes 12292
  9.5 28.5 %copy-start.30 = (bf16[512]{0:T(512)(128)(2,1)S(1)}, bf16[512]{0:T(512)(128)(2,1)}, u32[]{:S(2)}) copy-start(bf16[512]{0:T(512)(128)(2,1)} %param.24) | copy-start | bytes 3076
  9.5 33.1 %copy-start.31 = (bf16[512]{0:T(512)(128)(2,1)S(1)}, bf16[512]{0:T(512)(128)(2,1)}, u32[]{:S(2)}) copy-start(bf16[512]{0:T(512)(128)(2,1)} %param.23) | copy-start | bytes 3076
  9.5 37.6 %copy-start = (f32[1,128,1024]{2,1,0:T(8,128)S(1)}, f32[1,128,1024]{2,1,0:T(8,128)}, u32[]{:S(2)}) copy-start(f32[1,128,1024]{2,1,0:T(8,128)} %param.15) | copy-start | bytes 1572868
  9.5 37.8 %copy-start.12 = (f32[1,128,1024]{2,1,0:T(8,128)S(1)}, f32[1,128,1024]{2,1,0:T(8,128)}, u32[]{:S(2)}) copy-start(f32[1,128,1024]{2,1,0:T(8,128)} %param.29) | copy-start | bytes 1572868
  9.5 335.3 %all-gather.21.cloned.1.call-start = ((), (), s32[]{:S(2)}) async-start(), calls=%async_computation.9 | async-start | bytes 12582912 | tf_op jit(solution)/shard_map/all_gather | solution.py:140
  10.1 395.7 %reduce-scatter.9.cloned.1.call-start = ((), (), s32[]{:S(2)}) async-start(), calls=%async_computation.13 | async-start | bytes 786432
  106.7 18.1 %copy-start.5 = (bf16[256,1024]{0,1:T(8,128)(2,1)}, bf16[256,1024]{0,1:T(8,128)(2,1)S(1)}, u32[]{:S(2)}) copy-start(bf16[256,1024]{0,1:T(8,128)(2,1)S(1)} %copy.54) | copy-start | bytes 1572868
  106.8 17.3 %copy-start.19 = (bf16[128,1024]{0,1:T(8,128)(2,1)}, bf16[128,1024]{0,1:T(8,128)(2,1)S(1)}, u32[]{:S(2)}) copy-start(bf16[128,1024]{0,1:T(8,128)(2,1)S(1)} %copy.55) | copy-start | bytes 786436
  125.4 11.7 %copy-start.10 = (bf16[16,64,128]{2,1,0:T(8,128)(2,1)}, bf16[16,64,128]{2,1,0:T(8,128)(2,1)S(1)}, u32[]{:S(2)}) copy-start(bf16[16,64,128]{2,1,0:T(8,128)(2,1)S(1)} %convolution_convert_fusion.6) | copy-start | bytes 786436
  239.4 105.4 %copy-start.17 = (bf16[128,1024]{1,0:T(8,128)(2,1)S(1)}, bf16[128,1024]{1,0:T(8,128)(2,1)}, u32[]{:S(2)}) copy-start(bf16[128,1024]{1,0:T(8,128)(2,1)} %get-tuple-element.52) | copy-start | bytes 786436
  353.2 6.8 copy-start.13
  360.1 1.8 copy-start.1
  360.3 0.8 copy-start.3
  369.6 37.5 %reduce-scatter.7.cloned.1.call-start = ((), (), s32[]{:S(2)}) async-start(), calls=%async_computation.12 | async-start | bytes 786432
  389.3 103.2 %all-gather.25.cloned.1.call-start = ((), (), s32[]{:S(2)}) async-start(), calls=%async_computation.11 | async-start | bytes 3145728 | tf_op jit(solution)/shard_map/all_gather | solution.py:225
  390.0 107.4 %all-gather.23.cloned.1.call-start = ((), (), s32[]{:S(2)}) async-start(), calls=%async_computation.10 | async-start | bytes 2359296 | tf_op jit(solution)/shard_map/all_gather | solution.py:278
  405.8 5.2 copy-start.14
  407.0 5.1 copy-start.8
  407.0 8.6 %copy-start.11 = (bf16[16,64,128]{2,1,0:T(8,128)(2,1)S(1)}, bf16[16,64,128]{2,1,0:T(8,128)(2,1)}, u32[]{:S(2)}) copy-start(bf16[16,64,128]{2,1,0:T(8,128)(2,1)} %copy-done.10) | copy-start | bytes 786436
  408.9 19.0 %copy-start.2 = (bf16[128,4096]{1,0:T(8,128)(2,1)S(1)}, bf16[128,4096]{1,0:T(8,128)(2,1)}, u32[]{:S(2)}) copy-start(bf16[128,4096]{1,0:T(8,128)(2,1)} %get-tuple-element.59) | copy-start | bytes 3145732
  412.1 12.4 %all-to-all-start = ((bf16[128,2,512]{0,2,1:T(8,128)(2,1)}), bf16[128,2,512]{0,2,1:T(8,128)(2,1)S(1)}, u32[]{:S(2)}, u32[]{:S(2)}) async-start(bf16[128,2,512]{0,2,1:T(8,128)(2,1)} %add_convert_fusion), calls=%async_computation | async-start | bytes 524288 | tf_op jit(solution)/shard_map/all_to_all | solution.py:273
  424.5 3.5 copy-start.21
  424.5 12.2 %all-to-all-start.1 = ((bf16[128,2,512]{2,0,1:T(8,128)(2,1)}), bf16[128,2,512]{2,0,1:T(8,128)(2,1)S(1)}, u32[]{:S(2)}, u32[]{:S(2)}) async-start(bf16[128,2,512]{2,0,1:T(8,128)(2,1)} %copy.60), calls=%async_computation.1 | async-start | bytes 524288 | tf_op jit(solution)/shard_map/all_to_all | solution.py:274
  427.9 12.3 %copy-start.18 = (bf16[128,1024]{1,0:T(8,128)(2,1)S(1)}, bf16[128,1024]{1,0:T(8,128)(2,1)}, u32[]{:S(2)}) copy-start(bf16[128,1024]{1,0:T(8,128)(2,1)} %get-tuple-element.52) | copy-start | bytes 786436
  436.6 28.8 %copy-start.20 = (bf16[128,2,512]{2,0,1:T(8,128)(2,1)}, bf16[128,2,512]{2,0,1:T(8,128)(2,1)S(1)}, u32[]{:S(2)}) copy-start(bf16[128,2,512]{2,0,1:T(8,128)(2,1)S(1)} %all-to-all-done.1) | copy-start | bytes 786436
  436.6 47.3 %all-to-all-start.3 = ((bf16[128,2,2048]{2,0,1:T(8,128)(2,1)}), bf16[128,2,2048]{2,0,1:T(8,128)(2,1)S(1)}, u32[]{:S(2)}, u32[]{:S(2)}) async-start(bf16[128,2,2048]{2,0,1:T(8,128)(2,1)} %bitcast.105), calls=%async_computation.3 | async-start | bytes 2097152 | tf_op jit(solution)/shard_map/all_to_all | solution.py:221
  483.9 8.6 %all-to-all-start.2 = ((bf16[128,2,512]{2,0,1:T(8,128)(2,1)}), bf16[128,2,512]{2,0,1:T(8,128)(2,1)S(1)}, u32[]{:S(2)}, u32[]{:S(2)}) async-start(bf16[128,2,512]{2,0,1:T(8,128)(2,1)} %bitcast.130), calls=%async_computation.2 | async-start | bytes 524288 | tf_op jit(solution)/shard_map/all_to_all | solution.py:220
  487.4 247.4 %all-reduce.14.cloned.1.call-start = ((), (), s32[]{:S(2)}) async-start(), calls=%async_computation.14 | async-start | bytes 25165824 | tf_op jit(solution)/shard_map/psum | solution.py:299
  492.5 4.9 copy-start.15
  501.6 0.7 copy-start.32
  501.6 5.0 copy-start.33
  501.6 13.1 %slice-start = ((s8[6291456]{0:T(1024)(128)(4,1)}), s8[2097152]{0:T(1024)(128)(4,1)S(1)}, s32[]{:S(2)}) async-start(s8[6291456]{0:T(1024)(128)(4,1)} %bitcast.109), calls=%async_computation.15 | async-start | bytes 4194304
  508.6 5.9 copy-start.9
  508.6 6.1 slice-start.1
  508.6 6.1 copy-start.22
  508.6 6.1 copy-start.23
  514.7 77.4 %copy-start.4 = (f32[128,1024]{1,0:T(8,128)S(1)}, f32[128,1024]{1,0:T(8,128)}, u32[]{:S(2)}) copy-start(f32[128,1024]{1,0:T(8,128)} %copy-done.3) | copy-start | bytes 1572868
  734.7 5.5 copy-start.16
  734.7 7.1 copy-start.7
  741.8 4.5 copy-start.6
Sparse Core Ops, SparseCore 0:
  9.5 83.3 all-gather.14
  94.4 39.2 all-gather.16
  135.3 104.0 all-gather.18
  240.8 103.9 all-gather.20
  369.7 14.6 reduce-scatter.8
  389.4 14.6 reduce-scatter.6
  406.2 41.5 all-gather.24
  449.9 34.3 all-gather.22
  501.7 232.9 all-reduce.13
where the time goes:
time: 758 us; the launch traced here: 757 us
  waiting for transfers between devices  415 us (55%)
  blocking collectives  172 us (23%)
  matrix products  90.1 us (12%)
  other arithmetic  29.9 us (4%)
  local copies, waits for them, and re-layouts  20.3 us (3%)
  between operations  15.8 us (2%)
  starting transfers between devices  14.8 us (2%)
    psum x1, waiting for transfers between devices, per_device(): lax.psum(attn_shares[2].astype(jnp.bfloat16), 'rep').astype(jnp.float32)  141 us
    all_gather x1, waiting for transfers between devices, per_device(): lax.all_gather(w_up, 'grp', axis=0, tiled=True)  102 us
    all_gather x1, waiting for transfers between devices, per_device(): lax.all_gather(w_down, 'grp', axis=0, tiled=True)  98.4 us
    psum x1, blocking collectives, per_device(): lax.psum(attn_shares[0].astype(jnp.bfloat16), 'rep').astype(jnp.float32)  61 us
    all_gather x1, waiting for transfers between devices, per_device(): lax.all_gather(w_qkv, 'grp', axis=0, tiled=True)  44.5 us
    all_gather x1, blocking collectives, per_device(): lax.all_gather(cot_b, 'grp', axis=0, tiled=True)  23.4 us
  transfers between devices with their start and end apart: 13, of which 8 were waited for; matrix products, arithmetic and copies ran while one was open for 13% of the time, Pallas kernels for 0%

commit v1 on v0

v1 whole, which is shorter than its diff:
```python
import functools
import math

import jax
import jax.numpy as jnp
from jax import lax
from jax.experimental import pallas as pl
from jax.experimental.pallas import tpu as pltpu
from jax.sharding import PartitionSpec as P

HEADS = 16
HEAD_DIM = 64
BF = jnp.bfloat16
F32 = jnp.float32

NORM_EPS = 1e-05
GELU_COEF = math.sqrt(2.0 / math.pi)


def layer_norm_forward(residual_state, norm_gain, norm_shift):
    center = residual_state - jnp.mean(residual_state, axis=-1, keepdims=True)
    inv_std = lax.rsqrt(jnp.mean(center * center, axis=-1, keepdims=True) + NORM_EPS)
    normed = center * inv_std
    return (
        normed * norm_gain.astype(jnp.float32) + norm_shift.astype(jnp.float32),
        normed,
        inv_std,
    )


def layer_norm_backward(grad_norm, normed, inv_std, norm_gain):
    scaled = grad_norm * norm_gain.astype(jnp.float32)
    return inv_std * (
        scaled
        - jnp.mean(scaled, axis=-1, keepdims=True)
        - normed * jnp.mean(scaled * normed, axis=-1, keepdims=True)
    )


def gelu_parts(pre_act):
    inner_arg = GELU_COEF * (pre_act + 0.044715 * pre_act * pre_act * pre_act)
    tangent = jnp.tanh(inner_arg)
    gelu_value = 0.5 * pre_act * (1.0 + tangent)
    gelu_slope = 0.5 * (1.0 + tangent) + 0.5 * pre_act * (1.0 - tangent * tangent) * GELU_COEF * (
        1.0 + 3.0 * 0.044715 * pre_act * pre_act
    )
    return (gelu_value, gelu_slope)


def contract(x, y, dx, dy):
    return lax.dot_general(x, y, (((dx,), (dy,)), ((), ())), preferred_element_type=F32)


def probabilities(q, k, row_pos, col_pos):
    scores = contract(q, k, 1, 1) * HEAD_DIM ** (-0.5)
    scores = jnp.where(col_pos <= row_pos, scores, F32(-1e30))
    row_max = jnp.max(scores, axis=-1, keepdims=True)
    total = jnp.sum(jnp.exp(scores - row_max), axis=-1, keepdims=True)
    return jnp.exp(scores - (row_max + jnp.log(total)))


def forward_kernel(row_ref, col_ref, q_ref, k_ref, v_ref, ctx_ref):
    row_pos, col_pos = row_ref[...], col_ref[...]
    outs = []
    for lo in range(0, q_ref.shape[1], HEAD_DIM):
        head = slice(lo, lo + HEAD_DIM)
        prob = probabilities(q_ref[:, head], k_ref[:, head], row_pos, col_pos)
        outs.append(contract(prob.astype(BF), v_ref[:, head], 1, 0))
    ctx_ref[...] = jnp.concatenate(outs, axis=1).astype(BF)


def backward_kernel(
    row_ref, col_ref, q_ref, k_ref, v_ref, g_ref, dq_ref, dk_ref, dv_ref, bq_ref, bv_ref
):
    row_pos, col_pos = row_ref[...], col_ref[...]
    dq, dk, dv = [], [], []
    for lo in range(0, q_ref.shape[1], HEAD_DIM):
        head = slice(lo, lo + HEAD_DIM)
        q, k, v, g = q_ref[:, head], k_ref[:, head], v_ref[:, head], g_ref[:, head]
        prob = probabilities(q, k, row_pos, col_pos)
        grad_prob = contract(g, v, 1, 1)
        mean = jnp.sum(prob * grad_prob, axis=-1, keepdims=True)
        grad_score = (prob * (grad_prob - mean) * HEAD_DIM ** (-0.5)).astype(BF)
        dq.append(contract(grad_score, k, 1, 0))
        dk.append(contract(grad_score, q, 0, 0))
        dv.append(contract(prob.astype(BF), g, 0, 0))
    dq, dk, dv = (jnp.concatenate(part, axis=1) for part in (dq, dk, dv))
    dq_ref[...] = dq.astype(BF)
    dk_ref[...] = dk.astype(BF)
    dv_ref[...] = dv.astype(BF)
    bq_ref[...] = jnp.sum(dq, axis=0, keepdims=True)
    bv_ref[...] = jnp.sum(dv, axis=0, keepdims=True)


def attention_call(kernel, row_pos, col_pos, arrays, outs):
    tokens, width = arrays[0].shape
    block = 2 * HEAD_DIM if width % (2 * HEAD_DIM) == 0 else width

    def spec(rows):
        return pl.BlockSpec((rows, block), lambda i: (0, i))

    return pl.pallas_call(
        kernel,
        grid=(width // block,),
        in_specs=[
            pl.BlockSpec((tokens, 1), lambda i: (0, 0)),
            pl.BlockSpec((1, tokens), lambda i: (0, 0)),
        ]
        + [spec(tokens)] * len(arrays),
        out_specs=[spec(o[0]) for o in outs],
        out_shape=[jax.ShapeDtypeStruct((o[0], width), o[1]) for o in outs],
        compiler_params=pltpu.CompilerParams(vmem_limit_bytes=60 * 1024 * 1024),
        cost_estimate=pl.CostEstimate(
            flops=4 * len(arrays) * tokens * tokens * width,
            bytes_accessed=4 * len(arrays) * tokens * width,
            transcendentals=2 * tokens * tokens * width // HEAD_DIM,
        ),
    )(row_pos, col_pos, *arrays)


def per_device(
    stream_in,
    first_norm_gain,
    first_norm_bias,
    w_qkv,
    bias_q,
    bias_v,
    w_out,
    bias_out,
    second_norm_gain,
    second_norm_bias,
    w_up,
    bias_up,
    w_down,
    bias_down,
    cotangent,
):
    group = lax.axis_size("grp")
    me = lax.axis_index("grp")
    residual = stream_in[0]
    cot = cotangent[0]
    rows, width = residual.shape
    cols = width // group
    tokens = rows * group
    hid = w_up.shape[1] // group

    def other(r):
        return lax.rem(me + (r % group), group)

    def send(x, shift):
        return lax.ppermute(x, "grp", [(i, (i + shift) % group) for i in range(group)])

    def roll(x, r):
        r = (r % group) * rows
        return x if r == 0 else jnp.concatenate([x[r:], x[:r]], axis=0)

    def block(x, r):
        return x[r * rows : (r + 1) * rows]

    def column_block(x, index, size):
        return lax.dynamic_slice_in_dim(x, index * size, size, axis=1)

    def gather_rows(x):
        return jnp.concatenate([x] + [send(x, -r) for r in range(1, group)], axis=0)

    def rows_to_columns(x):
        parts = [column_block(x, me, cols)]
        parts += [send(column_block(x, other(-r), cols), -r) for r in range(1, group)]
        return jnp.concatenate(parts, axis=0)

    def sum_columns(x, weight_of):
        received = [
            send(contract(roll(x, r), weight_of(other(r)), 1, 0).astype(BF), r)
            for r in range(1, group)
        ]
        total = contract(x, weight_of(me), 1, 0)
        for part in received:
            total = total + part.astype(F32)
        return total

    def sum_rows(x, weight):
        received = [
            send(contract(block(x, r), weight, 1, 0).astype(BF), r) for r in range(1, group)
        ]
        total = contract(block(x, 0), weight, 1, 0)
        for part in received:
            total = total + part.astype(F32)
        return total

    def columns_to_rows(x):
        whole = jnp.zeros((rows, width), F32)
        whole = lax.dynamic_update_slice_in_dim(whole, block(x, 0), me * cols, axis=1)
        for r in range(1, group):
            part = send(block(x, r).astype(BF), r).astype(F32)
            whole = lax.dynamic_update_slice_in_dim(whole, part, other(-r) * cols, axis=1)
        return whole

    def gather_columns(x):
        parts = [x] + [send(roll(x, -r), -r) for r in range(1, group)]
        if group == 2:
            low = jnp.where(me == 0, parts[0], parts[1])
            high = jnp.where(me == 0, parts[1], parts[0])
            return jnp.stack([low, high], axis=-2)
        whole = jnp.zeros(x.shape[:-1] + (group, x.shape[-1]), x.dtype)
        for r, part in enumerate(parts):
            whole = lax.dynamic_update_slice_in_dim(
                whole, jnp.expand_dims(part, -2), other(r), axis=x.ndim - 1
            )
        return whole

    cot_b = cot.astype(BF)
    cot_full = gather_rows(cot_b)
    vectors = jnp.stack(
        [first_norm_gain, first_norm_bias, second_norm_gain, second_norm_bias, bias_out, bias_down]
    )
    vectors = lax.all_gather(vectors, "grp", axis=1, tiled=True)
    gain_one, shift_one, gain_two, shift_two, full_bo, full_bd = (vectors[i] for i in range(6))

    normalized, standard_one, inverse_one = layer_norm_forward(residual, gain_one, shift_one)
    act_one_cols = rows_to_columns(normalized.astype(BF))
    w3 = w_qkv.reshape(cols, 3, group, cols)
    qkv = sum_columns(
        act_one_cols,
        lambda d: lax.dynamic_index_in_dim(w3, d, axis=2, keepdims=False).reshape(cols, 3 * cols),
    )
    queries = (qkv[:, :cols] + bias_q.astype(F32)).astype(BF)
    keys = qkv[:, cols : 2 * cols].astype(BF)
    values = (qkv[:, 2 * cols :] + bias_v.astype(F32)).astype(BF)

    index = jnp.arange(tokens, dtype=jnp.int32)
    position = lax.rem(index + me * rows, tokens)
    row_pos, col_pos = position[:, None], position[None, :]
    (context,) = attention_call(
        forward_kernel, row_pos, col_pos, (queries, keys, values), [(tokens, BF)]
    )
    middle = residual + sum_rows(context, w_out) + full_bo.astype(F32)

    normalized, standard_two, inverse_two = layer_norm_forward(middle, gain_two, shift_two)
    act_two_cols = rows_to_columns(normalized.astype(BF))
    pre_act = sum_columns(act_two_cols, lambda d: column_block(w_up, d, hid)) + bias_up.astype(F32)
    gelu_value, gelu_slope = gelu_parts(pre_act)
    hidden = gelu_value.astype(BF)

    grad_pre = contract(cot_full, w_down, 1, 1) * gelu_slope
    grad_pre_b = grad_pre.astype(BF)
    d_bias_up = jnp.sum(grad_pre, axis=0)
    grad_pre_full = gather_columns(grad_pre_b).reshape(tokens, group * hid)
    d_w_down = contract(hidden, cot_full, 0, 0)
    total_w_down = lax.psum(d_w_down.astype(BF), "rep")
    result = middle + sum_rows(hidden, w_down) + full_bd.astype(F32)

    grad_act_cols = contract(grad_pre_full, w_up, 1, 1)
    d_shift_two = jnp.sum(grad_act_cols, axis=0)
    grad_act = columns_to_rows(grad_act_cols)
    d_w_up = contract(act_two_cols, grad_pre_full, 0, 0)
    total_w_up = lax.psum(d_w_up.astype(BF), "rep")
    d_gain_two = jnp.sum(grad_act * standard_two, axis=0)
    grad_middle = cot + layer_norm_backward(grad_act, standard_two, inverse_two, gain_two)

    grad_mid_full = gather_rows(grad_middle.astype(BF))
    grad_context = contract(grad_mid_full, w_out, 1, 1).astype(BF)
    d_w_out = contract(context, grad_mid_full, 0, 0)
    d_q, d_k, d_v, d_bias_q, d_bias_v = attention_call(
        backward_kernel,
        row_pos,
        col_pos,
        (queries, keys, values, grad_context),
        [(tokens, BF)] * 3 + [(1, F32)] * 2,
    )
    grad_proj = jnp.stack([d_q, d_k, d_v], axis=1)
    grad_proj_full = gather_columns(grad_proj).reshape(tokens, 3 * group * cols)
    grad_act_cols = contract(grad_proj_full, w_qkv, 1, 1)
    d_shift_one = jnp.sum(grad_act_cols, axis=0)
    grad_act = columns_to_rows(grad_act_cols)
    d_w_qkv = contract(act_one_cols, grad_proj_full, 0, 0)
    d_gain_one = jnp.sum(grad_act * standard_one, axis=0)
    input_gradient = grad_middle + layer_norm_backward(
        grad_act, standard_one, inverse_one, gain_one
    )
    total_w_out = lax.psum(d_w_out.astype(BF), "rep")
    total_w_qkv = lax.psum(d_w_qkv.astype(BF), "rep")

    sums = jnp.stack(
        [d_gain_one, d_gain_two, jnp.sum(grad_middle, axis=0), jnp.sum(cot, axis=0)]
    )
    mine = column_block(sums, me, cols)
    for r in range(1, group):
        mine = mine + send(column_block(sums, other(r), cols), r)
    owned = jnp.stack([d_shift_one, d_shift_two, d_bias_q[0], d_bias_v[0]])
    small = jnp.concatenate([mine.reshape(-1), owned.reshape(-1), d_bias_up])
    small = lax.psum(small, "rep")
    part = [small[i * cols : (i + 1) * cols] for i in range(8)]
    return (
        result[None],
        input_gradient[None],
        part[0],
        part[4],
        total_w_qkv.astype(F32),
        part[6],
        part[7],
        total_w_out.astype(F32),
        part[2],
        part[1],
        part[5],
        total_w_up.astype(F32),
        small[8 * cols :],
        total_w_down.astype(F32),
        part[3],
    )


def solution(mesh):
    return jax.shard_map(
        per_device,
        mesh=mesh,
        in_specs=(
            P("rep", "grp", None),
            P("grp"),
            P("grp"),
            P("grp", None),
            P("grp"),
            P("grp"),
            P("grp", None),
            P("grp"),
            P("grp"),
            P("grp"),
            P("grp", None),
            P("grp"),
            P("grp", None),
            P("grp"),
            P("rep", "grp", None),
        ),
        out_specs=(
            P("rep", "grp", None),
            P("rep", "grp", None),
            P("grp"),
            P("grp"),
            P("grp", None),
            P("grp"),
            P("grp"),
            P("grp", None),
            P("grp"),
            P("grp"),
            P("grp"),
            P("grp", None),
            P("grp"),
            P("grp", None),
            P("grp"),
        ),
        check_vma=False,
    )
```

time: 758 us -> 446 us (0.59)
  waiting for transfers between devices: 415 us -> 239 us
  blocking collectives: 172 us -> 66.5 us
  matrix products: 90.1 us -> 45.5 us
  Pallas kernels: 0 us -> 13.7 us
    all_gather x6 -> x0, waiting for transfers between devices: 254 us -> none  [the longest x1 102 us: per_device(): lax.all_gather(w_up, 'grp', axis=0, tiled=True)]
    all_gather x13 -> x1, blocking collectives: 103 us -> 5.31 us  [per_device(): vectors = lax.all_gather(vectors, 'grp', axis=1, tiled=True)]
    ppermute x0 -> x13, waiting for transfers between devices: none -> 81.2 us  [send(): lax.ppermute(x, 'grp', [(i, (i + shift) % group) for i in range(group)])]
    dot_general x18 -> x16, matrix products: 90.1 us -> 45.5 us  [contract(): lax.dot_general(x, y, (((dx,), (dy,)), ((), ())), preferred_element_type=...]
    all_to_all x4 -> x0, waiting for transfers between devices: 17.3 us -> none  [the longest x1 8.07 us: per_device(): lax.all_to_all(act_one, 'grp', split_axis=1, concat_axis=0, tiled=True)]
    psum x1, waiting for transfers between devices: 141 us -> 157 us  [per_device(): total_w_qkv = lax.psum(d_w_qkv.astype(BF), 'rep')]
    all_to_all x4 -> x0, starting transfers between devices: 13.9 us -> none  [the longest x1 3.58 us: per_device(): lax.all_to_all(hidden, 'grp', split_axis=1, concat_axis=0, tiled=True)]
    pallas_call x0 -> x2, Pallas kernels: none -> 13.7 us  [attention_call(): pl.pallas_call(kernel, grid=(width // block,), in_specs=[pl.BlockSpec((to...]
  transfers between devices with their start and end apart: 13 -> 14, of which waited for: 8 -> 11; matrix products, arithmetic and copies ran while one was open for 13% -> 10% of each run, Pallas kernels for 0% -> 0%
where the time goes in v1:
time: 446 us
  waiting for transfers between devices  239 us (54%)
  blocking collectives  66.5 us (15%)
  matrix products  45.5 us (10%)
  other arithmetic  32.2 us (7%)
  local copies, waits for them, and re-layouts  21.6 us (5%)
  between operations  14.6 us (3%)
  Pallas kernels  13.7 us (3%)
  starting transfers between devices  12.8 us (3%)
    psum x1, waiting for transfers between devices, per_device(): total_w_qkv = lax.psum(d_w_qkv.astype(BF), 'rep')  157 us
    ppermute x13, waiting for transfers between devices, send(): lax.ppermute(x, 'grp', [(i, (i + shift) % group) for i in range(group)])  81.2 us
    psum x1, blocking collectives, per_device(): small = lax.psum(small, 'rep')  61.2 us
    dot_general x16, matrix products, contract(): lax.dot_general(x, y, (((dx,), (dy,)), ((), ())), preferred_element_type=...  45.5 us
    pallas_call x2, Pallas kernels, attention_call(): pl.pallas_call(kernel, grid=(width // block,), in_specs=[pl.BlockSpec((to...  13.7 us
    ppermute x13, starting transfers between devices, send(): lax.ppermute(x, 'grp', [(i, (i + shift) % group) for i in range(group)])  12.8 us
  transfers between devices with their start and end apart: 14, of which 11 were waited for; matrix products, arithmetic and copies ran while one was open for 10% of the time, Pallas kernels for 0%

profile of v1, /device:TPU:0, one launch (start us, length us, event | category | flops | bytes accessed | tf_op | source)
XLA Modules:
  0.0 445.5 jit_solution(4957920168348651859)
XLA Ops:
  7.3 0.8 stack.75
  8.7 0.7 stack.77
  11.5 5.3 %all_gather.3 = bf16[6,1024]{1,0:T(8,128)(2,1)S(1)} all-gather(bf16[6,512]{1,0:T(8,128)(2,1)S(1)} %stack.81), channel_id=1, replica_groups=mesh['rep'=16,'grp'=2] {'grp'}, dimensions={1}, use_global_device_ids=true | all-gather | bytes 18432 | tf_op jit(solution)/shard_map/all_gather | solution.py:216
  17.4 1.2 reduce_sum.135
  18.6 1.2 multiply_reduce_fusion.5
  19.8 1.2 add_convert_fusion.1
  21.1 2.1 collective-permute-start
  23.2 4.6 %copy.32 = bf16[512,3072]{0,1:T(8,128)(2,1)} copy(bf16[512,3072]{1,0:T(8,128)(2,1)} %param.18) | data formatting | bytes 6291456 | tf_op args[3]
  27.8 2.1 constant_dynamic-slice_fusion.3
  29.9 1.5 convolution_convert_fusion.4
  32.1 0.7 negate_select_fusion.row_ref
  32.8 16.9 %collective-permute-done.1 = bf16[256,1536]{1,0:T(8,128)(2,1)} collective-permute-done((bf16[256,1536]{1,0:T(8,128)(2,1)}, bf16[256,1536]{1,0:T(8,128)(2,1)}, u32[]{:S(2)}, u32[]{:S(2)}) %collective-permute-start.1) | collective-permute-done | bytes 786464 | tf_op jit(solution)/shard_map/ppermute | solution.py:151
  49.6 1.7 convolution_add_fusion
  51.4 0.7 slice.180.k_ref
  52.1 0.9 fusion.11
  53.0 6.2 %shard_map.262 = bf16[256,512]{1,0:T(8,128)(2,1)} custom-call(s32[256,1]{1,0:T(8,128)} %negate_select_fusion.row_ref, s32[1,256]{1,0:T(1,128)} %compare_select_fusion.col_ref, bf16[256,512]{1,0:T(8,128)(2,1)} %get-tuple-element.46.q_ref, bf16[256,512]{1,0:T(8,128)(2,1)} %slice.180.k_ref, bf16[256,512]{1,0:T(8,128)(2,1)} %get-tuple-element.45.v_ref), custom_call_target="tpu_custom_call" | custom-call | flops 402653184 | bytes 1572864 | tf_op jit(solution)/shard_map/pallas_call | solution.py:102
  59.2 1.2 convolution_convert_fusion.7
  60.8 6.1 %collective-permute-done.2 = bf16[128,1024]{1,0:T(8,128)(2,1)S(1)} collective-permute-done((bf16[128,1024]{1,0:T(8,128)(2,1)S(1)}, bf16[128,1024]{1,0:T(8,128)(2,1)S(1)}, u32[]{:S(2)}, u32[]{:S(2)}) %collective-permute-start.2) | collective-permute-done | bytes 262176 | tf_op jit(solution)/shard_map/ppermute | solution.py:151
  66.9 1.3 fusion.46
  69.5 4.7 %collective-permute-done.3 = bf16[128,512]{1,0:T(8,128)(2,1)S(1)} collective-permute-done((bf16[128,512]{1,0:T(8,128)(2,1)S(1)}, bf16[128,512]{1,0:T(8,128)(2,1)S(1)}, u32[]{:S(2)}, u32[]{:S(2)}) %collective-permute-start.3) | collective-permute-done | bytes 131104 | tf_op jit(solution)/shard_map/ppermute | solution.py:151
  74.2 3.3 convolution_convert_fusion.3
  77.8 0.8 fusion.44
  78.6 1.7 collective-permute-start.6
  80.9 20.0 %collective-permute-done.4 = bf16[256,2048]{1,0:T(8,128)(2,1)} collective-permute-done((bf16[256,2048]{1,0:T(8,128)(2,1)}, bf16[256,2048]{1,0:T(8,128)(2,1)}, u32[]{:S(2)}, u32[]{:S(2)}) %collective-permute-start.4) | collective-permute-done | bytes 1048608 | tf_op jit(solution)/shard_map/ppermute | solution.py:151
  100.9 3.1 multiply_convert_fusion
  104.1 4.0 fusion.41
  108.2 1.2 pad_maximum_fusion.2
  110.0 3.7 convolution_convert_fusion.8
  113.7 1.4 collective-permute-start.5
  115.2 16.5 %collective-permute-done.7 = bf16[256,2048]{1,0:T(8,128)(2,1)} collective-permute-done((bf16[256,2048]{1,0:T(8,128)(2,1)}, bf16[256,2048]{1,0:T(8,128)(2,1)}, u32[]{:S(2)}, u32[]{:S(2)}) %collective-permute-start.7) | collective-permute-done | bytes 1048608 | tf_op jit(solution)/shard_map/ppermute | solution.py:151
  131.7 1.4 select_bitcast_fusion.1
  133.0 1.5 pad_maximum_fusion
  134.5 3.9 copy.33
  138.5 4.9 %fusion.47 = (f32[512]{0:T(512)}, f32[256,512]{1,0:T(8,128)S(1)}) fusion(bf16[256,4096]{0,1:T(8,128)(2,1)} %bitcast.76, bf16[512,4096]{1,0:T(8,128)(2,1)} %param.25), kind=kOutput, calls=%fused_computation.128 | convolution fusion | flops 1073872384 | bytes 6817792 | tf_op jit(solution)/shard_map/dot_general | solution.py:51
  143.4 0.9 collective-permute-start.8
  144.4 5.0 %collective-permute-done.8 = bf16[128,512]{1,0:T(8,128)(2,1)S(1)} collective-permute-done((bf16[128,512]{1,0:T(8,128)(2,1)S(1)}, bf16[128,512]{1,0:T(8,128)(2,1)S(1)}, u32[]{:S(2)}, u32[]{:S(2)}) %collective-permute-start.8) | collective-permute-done | bytes 131104 | tf_op jit(solution)/shard_map/ppermute | solution.py:151
  149.5 0.8 multiply_reduce_fusion
  150.3 3.2 fusion.40
  153.5 0.8 copy-done.7
  154.4 1.2 collective-permute-start.9
  155.6 5.2 %collective-permute-done.9 = bf16[128,1024]{1,0:T(8,128)(2,1)S(1)} collective-permute-done((bf16[128,1024]{1,0:T(8,128)(2,1)S(1)}, bf16[128,1024]{1,0:T(8,128)(2,1)S(1)}, u32[]{:S(2)}, u32[]{:S(2)}) %collective-permute-start.9) | collective-permute-done | bytes 262176 | tf_op jit(solution)/shard_map/ppermute | solution.py:151
  160.8 1.2 convolution_convert_fusion.6.g_ref
  162.0 7.5 %shard_map.263 = (bf16[256,512]{1,0:T(8,128)(2,1)}, bf16[256,512]{1,0:T(8,128)(2,1)}, bf16[256,512]{1,0:T(8,128)(2,1)}, f32[1,512]{1,0:T(1,128)}, f32[1,512]{1,0:T(1,128)}) custom-call(s32[256,1]{1,0:T(8,128)} %negate_select_fusion.row_ref, s32[1,256]{1,0:T(1,128)} %compare_select_fusion.col_ref, bf16[256,512]{1,0:T(8,128)(2,1)} %get-tuple-element.46.q_ref, ...), custom_call_target="tpu_custom_call" | custom-call | flops 536870912 | bytes 2097152 | tf_op jit(solution)/shard_map/pallas_call | solution.py:102
  169.5 1.2 pad_maximum_fusion.3
  170.9 1.2 collective-permute-start.10
  172.1 4.3 convolution_convert_fusion.2
  176.5 3.3 convolution_convert_fusion
  179.8 1.5 convolution_convert_fusion.5
  181.3 1.6 collective-permute-done.10
  183.2 1.6 copy.34
  184.8 4.1 convolution_convert_fusion.1
  188.9 1.4 copy-done.6
  190.3 3.0 fusion.48
  193.4 1.2 collective-permute-start.11
  194.7 3.7 collective-permute-done.11
  198.8 1.2 collective-permute-start.12
  200.0 1.0 add_bitcast_fusion
  201.0 1.5 collective-permute-done.12
  202.5 61.2 %psum.35 = f32[6144]{0:T(1024)S(1)} all-reduce(f32[6144]{0:T(1024)S(1)} %pad_maximum_fusion.17), channel_id=1, replica_groups=mesh['rep'=16,'grp'=2] {'rep'}, use_global_device_ids=true, to_apply=%region_15.16 | all-reduce | flops 6144 | bytes 49152 | tf_op jit(solution)/shard_map/psum | solution.py:291
  264.9 157.4 %all-reduce.3.cloned.1.call-done = (bf16[512,3072]{1,0:T(8,128)(2,1)}, bf16[512,1024]{1,0:T(8,128)(2,1)}, bf16[512,4096]{1,0:T(8,128)(2,1)}, bf16[2048,1024]{1,0:T(8,128)(2,1)}) async-done(((bf16[512,3072]{1,0:T(8,128)(2,1)}, bf16[512,1024]{1,0:T(8,128)(2,1)}, bf16[512,4096]{1,0:T(8,128)(2,1)}, bf16[2048,1024]{1,0:T(8,128)(2,1)}), (bf16[512,3072]{1,0:T(8,128)(2,1)}, bf16[512,1024]{1,0:T(8,128)(2,1)}, ...) | async-done | bytes 12582928 | tf_op jit(solution)/shard_map/psum | solution.py:281
  422.3 6.8 %convert_element_type.134 = f32[512,4096]{1,0:T(8,128)} convert(bf16[512,4096]{1,0:T(8,128)(2,1)} %get-tuple-element.33) | non-fusion elementwise | flops 2097152 | bytes 12582912 | tf_op jit(solution)/shard_map/convert_element_type | solution.py:305
  429.2 4.4 convert_element_type.136
  433.6 3.5 convert_element_type.130
  437.1 1.6 convert_element_type.132
  (137 shorter events, 9.6 us)
Async XLA Ops:
  7.2 52.0 %copy-start = (bf16[512,1024]{1,0:T(8,128)(2,1)S(1)}, bf16[512,1024]{1,0:T(8,128)(2,1)}, u32[]{:S(2)}) copy-start(bf16[512,1024]{1,0:T(8,128)(2,1)} %param.21) | copy-start | bytes 3145732
  7.2 415.1 %all-reduce.3.cloned.1.call-start = ((), (), s32[]{:S(2)}) async-start(), calls=%async_computation | async-start | bytes 25165824 | tf_op jit(solution)/shard_map/psum | solution.py:281
  18.5 9.3 %copy-start.28 = (f32[128]{0:T(128)}, f32[128]{0:T(128)S(1)}, u32[]{:S(2)}) copy-start(f32[128]{0:T(128)S(1)} %broadcast_multiply_fusion.5) | copy-start | bytes 1540
  19.8 8.0 %copy-start.32 = (f32[128]{0:T(128)}, f32[128]{0:T(128)S(1)}, u32[]{:S(2)}) copy-start(f32[128]{0:T(128)S(1)} %add_rsqrt_fusion.1) | copy-start | bytes 1540
  21.1 8.9 %collective-permute-start = (bf16[128,512]{1,0:T(8,128)(2,1)S(1)}, bf16[128,512]{1,0:T(8,128)(2,1)S(1)}, u32[]{:S(2)}, u32[]{:S(2)}) collective-permute-start(bf16[128,512]{1,0:T(8,128)(2,1)S(1)} %get-tuple-element.56), channel_id=1, source_target_pairs={{0,1},{1,0},{2,3},{3,2},{4,5},{5,4},{6,7},{7,6},{8,9},{9,8},{10,11... | collective-permute-start | bytes 393224 | tf_op jit(solution)/shard_map/ppermute | solution.py:151
  29.9 1.6 copy-start.40
  29.9 1.6 copy-start.41
  31.5 18.2 %collective-permute-start.1 = (bf16[256,1536]{1,0:T(8,128)(2,1)}, bf16[256,1536]{1,0:T(8,128)(2,1)}, u32[]{:S(2)}, u32[]{:S(2)}) collective-permute-start(bf16[256,1536]{1,0:T(8,128)(2,1)} %convolution_convert_fusion.4), channel_id=1, source_target_pairs={{0,1},{1,0},{2,3},{3,2},{4,5},{5,4},{6,7},{7,6},{8,9},{9,8},{10,11... | collective-permute-start | bytes 2359304 | tf_op jit(solution)/shard_map/ppermute | solution.py:151
  53.0 13.8 %copy-start.2 = (f32[1,128,1024]{2,1,0:T(8,128)S(1)}, f32[1,128,1024]{2,1,0:T(8,128)}, u32[]{:S(2)}) copy-start(f32[1,128,1024]{2,1,0:T(8,128)} %param.15) | copy-start | bytes 1572868
  53.0 13.8 %copy-start.24 = (f32[1,1024]{1,0:T(1,128)S(1)}, f32[1,1024]{1,0:T(1,128)}, u32[]{:S(2)}) copy-start(f32[1,1024]{1,0:T(1,128)} %get-tuple-element.69) | copy-start | bytes 12292
  60.4 6.4 %collective-permute-start.2 = (bf16[128,1024]{1,0:T(8,128)(2,1)S(1)}, bf16[128,1024]{1,0:T(8,128)(2,1)S(1)}, u32[]{:S(2)}, u32[]{:S(2)}) collective-permute-start(bf16[128,1024]{1,0:T(8,128)(2,1)S(1)} %convolution_convert_fusion.7), channel_id=1, source_target_pairs={{0,1},{1,0},{2,3},{3,2},{4,5},{5,4},{6,7},{7,6},{8,9},{9,8},{10,11... | collective-permute-start | bytes 786440 | tf_op jit(solution)/shard_map/ppermute | solution.py:151
  68.2 0.5 copy-start.30
  68.4 0.5 copy-start.34
  69.1 8.7 %copy-start.13 = (f32[1,128,1024]{2,1,0:T(8,128)S(1)}, f32[1,128,1024]{2,1,0:T(8,128)}, u32[]{:S(2)}) copy-start(f32[1,128,1024]{2,1,0:T(8,128)} %param.29) | copy-start | bytes 1572868
  69.1 5.0 %collective-permute-start.3 = (bf16[128,512]{1,0:T(8,128)(2,1)S(1)}, bf16[128,512]{1,0:T(8,128)(2,1)S(1)}, u32[]{:S(2)}, u32[]{:S(2)}) collective-permute-start(bf16[128,512]{1,0:T(8,128)(2,1)S(1)} %get-tuple-element.54), channel_id=1, source_target_pairs={{0,1},{1,0},{2,3},{3,2},{4,5},{5,4},{6,7},{7,6},{8,9},{9,8},{10,11... | collective-permute-start | bytes 393224 | tf_op jit(solution)/shard_map/ppermute | solution.py:151
  74.2 4.4 copy-start.20
  74.2 6.1 %copy-start.36 = (bf16[2048]{0:T(1024)(128)(2,1)S(1)}, bf16[2048]{0:T(1024)(128)(2,1)}, u32[]{:S(2)}) copy-start(bf16[2048]{0:T(1024)(128)(2,1)} %param.26) | copy-start | bytes 12292
  77.5 23.4 %collective-permute-start.4 = (bf16[256,2048]{1,0:T(8,128)(2,1)}, bf16[256,2048]{1,0:T(8,128)(2,1)}, u32[]{:S(2)}, u32[]{:S(2)}) collective-permute-start(bf16[256,2048]{1,0:T(8,128)(2,1)} %convolution_convert_fusion.3), channel_id=1, source_target_pairs={{0,1},{1,0},{2,3},{3,2},{4,5},{5,4},{6,7},{7,6},{8,9},{9,8},{10,11... | collective-permute-start | bytes 3145736 | tf_op jit(solution)/shard_map/ppermute | solution.py:151
  78.6 25.5 %collective-permute-start.6 = (bf16[128,1024]{1,0:T(8,128)(2,1)}, bf16[128,1024]{1,0:T(8,128)(2,1)}, u32[]{:S(2)}, u32[]{:S(2)}) collective-permute-start(bf16[128,1024]{1,0:T(8,128)(2,1)} %get-tuple-element.52), channel_id=1, source_target_pairs={{0,1},{1,0},{2,3},{3,2},{4,5},{5,4},{6,7},{7,6},{8,9},{9,8},{10,11... | collective-permute-start | bytes 786440 | tf_op jit(solution)/shard_map/ppermute | solution.py:151
  80.9 23.2 %copy-start.3 = (bf16[2048,1024]{1,0:T(8,128)(2,1)S(1)}, bf16[2048,1024]{1,0:T(8,128)(2,1)}, u32[]{:S(2)}) copy-start(bf16[2048,1024]{1,0:T(8,128)(2,1)} %param.27) | copy-start | bytes 12582916
  108.1 1.3 copy-start.10
  109.4 22.2 %collective-permute-start.7 = (bf16[256,2048]{1,0:T(8,128)(2,1)}, bf16[256,2048]{1,0:T(8,128)(2,1)}, u32[]{:S(2)}, u32[]{:S(2)}) collective-permute-start(bf16[256,2048]{1,0:T(8,128)(2,1)} %pad_maximum_fusion.2), channel_id=1, source_target_pairs={{0,1},{1,0},{2,3},{3,2},{4,5},{5,4},{6,7},{7,6},{8,9},{9,8},{10,11... | collective-permute-start | bytes 3145736 | tf_op jit(solution)/shard_map/ppermute | solution.py:151
  110.0 21.7 %copy-start.11 = (bf16[256,2048]{1,0:T(8,128)(2,1)S(1)}, bf16[256,2048]{1,0:T(8,128)(2,1)}, u32[]{:S(2)}) copy-start(bf16[256,2048]{1,0:T(8,128)(2,1)} %copy-done.10) | copy-start | bytes 3145732
  113.7 36.6 %collective-permute-start.5 = (bf16[128,1024]{1,0:T(8,128)(2,1)}, bf16[128,1024]{1,0:T(8,128)(2,1)}, u32[]{:S(2)}, u32[]{:S(2)}) collective-permute-start(bf16[128,1024]{1,0:T(8,128)(2,1)} %convolution_convert_fusion.8), channel_id=1, source_target_pairs={{0,1},{1,0},{2,3},{3,2},{4,5},{5,4},{6,7},{7,6},{8,9},{9,8},{10,11... | collective-permute-start | bytes 786440 | tf_op jit(solution)/shard_map/ppermute | solution.py:151
  138.5 11.0 %copy-start.31 = (f32[128]{0:T(128)S(1)}, f32[128]{0:T(128)}, u32[]{:S(2)}) copy-start(f32[128]{0:T(128)} %copy-done.30) | copy-start | bytes 1540
  138.5 11.0 %copy-start.35 = (f32[128]{0:T(128)S(1)}, f32[128]{0:T(128)}, u32[]{:S(2)}) copy-start(f32[128]{0:T(128)} %copy-done.34) | copy-start | bytes 1540
  138.5 11.8 %copy-start.4 = (bf16[2048,1024]{1,0:T(8,128)(2,1)S(1)}, bf16[2048,1024]{1,0:T(8,128)(2,1)}, u32[]{:S(2)}) copy-start(bf16[2048,1024]{1,0:T(8,128)(2,1)} %param.27) | copy-start | bytes 12582916
  143.3 6.9 %copy-start.14 = (f32[1,128,1024]{2,1,0:T(8,128)S(1)}, f32[1,128,1024]{2,1,0:T(8,128)}, u32[]{:S(2)}) copy-start(f32[1,128,1024]{2,1,0:T(8,128)} %param.29) | copy-start | bytes 1572868
  143.4 6.1 %collective-permute-start.8 = (bf16[128,512]{1,0:T(8,128)(2,1)S(1)}, bf16[128,512]{1,0:T(8,128)(2,1)S(1)}, u32[]{:S(2)}, u32[]{:S(2)}) collective-permute-start(bf16[128,512]{1,0:T(8,128)(2,1)S(1)} %slice.182), channel_id=1, source_target_pairs={{0,1},{1,0},{2,3},{3,2},{4,5},{5,4},{6,7},{7,6},{8,9},{9,8},{10,11... | collective-permute-start | bytes 393224 | tf_op jit(solution)/shard_map/ppermute | solution.py:151
  153.5 0.8 copy-start.7
  154.4 6.4 %collective-permute-start.9 = (bf16[128,1024]{1,0:T(8,128)(2,1)S(1)}, bf16[128,1024]{1,0:T(8,128)(2,1)S(1)}, u32[]{:S(2)}, u32[]{:S(2)}) collective-permute-start(bf16[128,1024]{1,0:T(8,128)(2,1)S(1)} %convert_element_type.126), channel_id=1, source_target_pairs={{0,1},{1,0},{2,3},{3,2},{4,5},{5,4},{6,7},{7,6},{8,9},{9,8},{10,11... | collective-permute-start | bytes 786440 | tf_op jit(solution)/shard_map/ppermute | solution.py:151
  160.8 8.7 %copy-start.22 = (bf16[128,1024]{1,0:T(8,128)(2,1)}, bf16[128,1024]{1,0:T(8,128)(2,1)S(1)}, u32[]{:S(2)}) copy-start(bf16[128,1024]{1,0:T(8,128)(2,1)S(1)} %collective-permute-done.9) | copy-start | bytes 786436
  170.8 5.6 %copy-start.5 = (bf16[256,2,2048]{0,2,1:T(8,128)(2,1)S(1)}, bf16[256,2,2048]{0,2,1:T(8,128)(2,1)}, u32[]{:S(2)}) copy-start(bf16[256,2,2048]{0,2,1:T(8,128)(2,1)} %copy.33) | copy-start | bytes 6291460
  170.9 5.6 %copy-start.21 = (bf16[128,512]{1,0:T(8,128)(2,1)S(1)}, bf16[128,512]{1,0:T(8,128)(2,1)}, u32[]{:S(2)}) copy-start(bf16[128,512]{1,0:T(8,128)(2,1)} %copy-done.20) | copy-start | bytes 393220
  170.9 12.1 %collective-permute-start.10 = (bf16[256,3,512]{2,0,1:T(8,128)(2,1)S(1)}, bf16[256,3,512]{2,0,1:T(8,128)(2,1)S(1)}, u32[]{:S(2)}, u32[]{:S(2)}) collective-permute-start(bf16[256,3,512]{2,0,1:T(8,128)(2,1)S(1)} %pad_maximum_fusion.4), channel_id=1, source_target_pairs={{0,1},{1,0},{2,3},{3,2},{4,5},{5,4},{6,7},{7,6},{8,9},{9,8},{10,11... | collective-permute-start | bytes 2359304 | tf_op jit(solution)/shard_map/ppermute | solution.py:151
  176.4 3.4 copy-start.16
  176.4 3.4 copy-start.23
  176.4 6.5 %copy-start.17 = (bf16[256,512]{1,0:T(8,128)(2,1)S(1)}, bf16[256,512]{1,0:T(8,128)(2,1)}, u32[]{:S(2)}) copy-start(bf16[256,512]{1,0:T(8,128)(2,1)} %get-tuple-element.20) | copy-start | bytes 786436
  176.5 6.5 %copy-start.18 = (bf16[256,512]{1,0:T(8,128)(2,1)S(1)}, bf16[256,512]{1,0:T(8,128)(2,1)}, u32[]{:S(2)}) copy-start(bf16[256,512]{1,0:T(8,128)(2,1)} %get-tuple-element.21) | copy-start | bytes 786436
  176.5 6.5 %copy-start.19 = (bf16[256,512]{1,0:T(8,128)(2,1)S(1)}, bf16[256,512]{1,0:T(8,128)(2,1)}, u32[]{:S(2)}) copy-start(bf16[256,512]{1,0:T(8,128)(2,1)} %get-tuple-element.22) | copy-start | bytes 786436
  188.9 1.4 copy-start.6
  190.3 4.3 copy-start.37
  190.3 4.3 copy-start.38
  190.3 4.3 copy-start.39
  190.3 8.1 %copy-start.29 = (f32[128]{0:T(128)S(1)}, f32[128]{0:T(128)}, u32[]{:S(2)}) copy-start(f32[128]{0:T(128)} %copy-done.28) | copy-start | bytes 1540
  190.3 8.1 %copy-start.33 = (f32[128]{0:T(128)S(1)}, f32[128]{0:T(128)}, u32[]{:S(2)}) copy-start(f32[128]{0:T(128)} %copy-done.32) | copy-start | bytes 1540
  193.3 5.4 %copy-start.25 = (f32[1024]{0:T(1024)S(1)}, f32[1024]{0:T(1024)}, u32[]{:S(2)}) copy-start(f32[1024]{0:T(1024)} %get-tuple-element.27) | copy-start | bytes 12292
  193.3 5.4 %copy-start.26 = (f32[1024]{0:T(1024)S(1)}, f32[1024]{0:T(1024)}, u32[]{:S(2)}) copy-start(f32[1024]{0:T(1024)} %get-tuple-element.35) | copy-start | bytes 12292
  193.3 6.7 %copy-start.8 = (f32[128,1024]{1,0:T(8,128)S(1)}, f32[128,1024]{1,0:T(8,128)}, u32[]{:S(2)}) copy-start(f32[128,1024]{1,0:T(8,128)} %copy-done.7) | copy-start | bytes 1572868
  193.4 5.0 %collective-permute-start.11 = (bf16[128,512]{1,0:T(8,128)(2,1)S(1)}, bf16[128,512]{1,0:T(8,128)(2,1)S(1)}, u32[]{:S(2)}, u32[]{:S(2)}) collective-permute-start(bf16[128,512]{1,0:T(8,128)(2,1)S(1)} %slice.181), channel_id=1, source_target_pairs={{0,1},{1,0},{2,3},{3,2},{4,5},{5,4},{6,7},{7,6},{8,9},{9,8},{10,11... | collective-permute-start | bytes 393224 | tf_op jit(solution)/shard_map/ppermute | solution.py:151
  194.7 7.8 %copy-start.27 = (f32[2048]{0:T(1024)S(1)}, f32[2048]{0:T(1024)}, u32[]{:S(2)}) copy-start(f32[2048]{0:T(1024)} %get-tuple-element.39) | copy-start | bytes 24580
  198.8 3.7 collective-permute-start.12
  422.3 6.8 %copy-start.9 = (bf16[2048,1024]{1,0:T(8,128)(2,1)S(1)}, bf16[2048,1024]{1,0:T(8,128)(2,1)}, u32[]{:S(2)}) copy-start(bf16[2048,1024]{1,0:T(8,128)(2,1)} %get-tuple-element.34) | copy-start | bytes 12582916
  429.2 4.4 copy-start.12
  433.6 3.5 copy-start.15
  433.6 5.1 %copy-start.1 = (bf16[512,1024]{1,0:T(8,128)(2,1)S(1)}, bf16[512,1024]{1,0:T(8,128)(2,1)}, u32[]{:S(2)}) copy-start(bf16[512,1024]{1,0:T(8,128)(2,1)} %param.21) | copy-start | bytes 3145732
Sparse Core Ops, SparseCore 0:
  189.0 233.2 all-reduce.2
